TPU v7x, 128 devices: a whole 4x4x4 slice. The times are simulated.
128 devices in a mesh: ckpt: 4 (over z_hi, core), space: 32 (over y, x, z_lo).
Axes of the slice: x: 4, y: 4, z: 4 (z_hi: 2, z_lo: 2; z = z_hi * 2 + z_lo), core: 2. Of those that a mesh axis runs over, the one named last changes fastest.
Arguments:
- checkpoint: float32 [32, 6, 16, 16, 128], P('space', None, 'ckpt'), may hold values from -5 to 5
- seeds: float32 [4, 32, 6, 16, 16, 128], P('ckpt', 'space'), may hold values from -6 to 6
- cell_rate: float32 [32, 16, 16, 128], P('space'), may hold values from 0.5 to 2
- flux_mats: float32 [3, 6, 6], replicated, may hold values from -1.25 to 1.25
- owner: int32 [32], replicated, may hold values from 0 to 31, each once
- neighbours: int32 [32, 6], replicated, may hold values from 0 to 31, as said below
- orientation: int32 [32, 6], replicated, may hold values from 0 to 3, as said below
Outputs:
- adjoint: float32 [4, 32, 6, 16, 16, 128], P('ckpt', 'space')
- final_state: float32 [32, 6, 16, 16, 128], P('space')
Inputs may be any that keep to these rules, and one draw needn't show every extreme that they name: owner lists each space index once. The block across the -x face of neighbours[b, 0] is b, across the +x face of neighbours[b, 1] is b, and likewise for y and z; a block may be its own neighbour. orientation[b, f] equals the code of the same face seen from the block across it.
All inputs are finite; a program needn't handle non-finite values.
Results may differ from a plain program's by a relative error of at most 0.0001.
Values sent between devices are 32-bit elements; how exact they have to be, the bound alone decides.
A program may use at most 128 MiB of HBM per device.

v0:
```python
import jax
import jax.numpy as jnp
from jax import lax
from jax.sharding import PartitionSpec as P

STEPS = 2
time_step = 0.05
damping = 0.015


def boundary(field, side):
    layer_axis = field.ndim - 3 + side // 2
    location = field.shape[layer_axis] - 1 if side % 2 == 0 else 0
    return lax.index_in_dim(field, location, layer_axis, keepdims=False)


def reorient(face, flips):
    face = jnp.where(flips % 2 == 1, jnp.flip(face, -2), face)
    return jnp.where(flips // 2 % 2 == 1, jnp.flip(face, -1), face)


def pad_with(field, ghosts):
    padded = jnp.pad(field, [(0, 0)] + [(1, 1)] * 3)
    for side in range(6):
        layer_axis = side // 2
        location = padded.shape[layer_axis + 1] - 1 if side % 2 == 0 else 0
        if layer_axis == 0:
            padded = padded.at[:, location, 1:-1, 1:-1].set(ghosts[side])
        elif layer_axis == 1:
            padded = padded.at[:, 1:-1, location, 1:-1].set(ghosts[side])
        else:
            padded = padded.at[:, 1:-1, 1:-1, location].set(ghosts[side])
    return padded


def ghost_layer(padded, side):
    layer_axis = side // 2
    location = padded.shape[layer_axis + 1] - 1 if side % 2 == 0 else 0
    if layer_axis == 0:
        return padded[:, location, 1:-1, 1:-1]
    if layer_axis == 1:
        return padded[:, 1:-1, location, 1:-1]
    return padded[:, 1:-1, 1:-1, location]


def add_layer(field, side, layer):
    layer_axis = side // 2
    location = field.shape[layer_axis + 1] - 1 if side % 2 == 0 else 0
    if layer_axis == 0:
        return field.at[:, location].add(layer)
    if layer_axis == 1:
        return field.at[:, :, location].add(layer)
    return field.at[:, :, :, location].add(layer)


def advance(padded, rates, flux_mats):
    interior = padded[:, 1:-1, 1:-1, 1:-1]
    divergence = jnp.zeros_like(interior)
    for direction in range(3):
        if direction == 0:
            strip = padded[:, :, 1:-1, 1:-1]
        elif direction == 1:
            strip = padded[:, 1:-1, :, 1:-1]
        else:
            strip = padded[:, 1:-1, 1:-1, :]
        length = strip.shape[direction + 1]
        left_cells = lax.slice_in_dim(strip, 0, length - 1, axis=direction + 1)
        right_cells = lax.slice_in_dim(strip, 1, length, axis=direction + 1)
        average = 0.5 * (left_cells + right_cells)
        difference = right_cells - left_cells
        spread = jnp.sqrt(1.0 + average[0] * average[0])
        face_flux = (
            jnp.einsum(
                "ij,jxyz->ixyz", flux_mats[direction], average, precision=lax.Precision.HIGHEST
            )
            - 0.5 * spread * difference
        )
        count = face_flux.shape[direction + 1]
        divergence = (
            divergence
            + lax.slice_in_dim(face_flux, 1, count, axis=direction + 1)
            - lax.slice_in_dim(face_flux, 0, count - 1, axis=direction + 1)
        )
    return interior - time_step * rates * divergence - damping * jnp.tanh(interior)


def pick(pieces, sources):
    count = pieces[0].shape[0]
    positions = jnp.arange(count, dtype=jnp.int32)
    result = []
    for side in range(6):
        weight = (positions == sources[side]).astype(jnp.float32)
        piece = pieces[side // 2][:, 1 - side % 2]
        result.append(jnp.sum(weight.reshape((count, 1, 1, 1)) * piece, axis=0))
    return tuple(result)


def side_pairs(layers):
    return [jnp.stack([layers[2 * pair], layers[2 * pair + 1]])[None] for pair in range(3)]


def on_device(checkpoint, seeds, cell_rate, flux_mats, owner, neighbours, orientation):
    restored = lax.all_gather(checkpoint, "ckpt", axis=2, tiled=True)[0]
    rates = cell_rate[0]
    block_count = owner.shape[0]
    indices = jnp.arange(block_count, dtype=jnp.int32)
    position = lax.axis_index("space")
    own_block = jnp.sum(jnp.where(owner == position, indices, 0))
    chosen = (indices == own_block).astype(jnp.int32)[:, None]
    across = jnp.sum(chosen * neighbours, axis=0)
    flips = jnp.sum(chosen * orientation, axis=0)
    sources = jnp.sum(
        (indices[None, :] == across[:, None]).astype(jnp.int32) * owner[None, :], axis=1
    )

    def gather_step(pieces):
        return pick(pieces, sources)

    def fetch(field):
        layers = [boundary(field, side) for side in range(6)]
        x_faces, y_faces, z_faces = side_pairs(layers)
        whole = gather_step(
            (
                lax.all_gather(x_faces, "space", axis=0, tiled=True),
                lax.all_gather(y_faces, "space", axis=0, tiled=True),
                lax.all_gather(z_faces, "space", axis=0, tiled=True),
            )
        )
        return [reorient(whole[side], flips[side]) for side in range(6)]

    padded_states = []
    state = restored
    for section in range(STEPS):
        padded = pad_with(state, fetch(state))
        padded_states.append(padded)
        state = advance(padded, rates, flux_mats)
    adjoint_now = seeds[0, 0]
    for section in reversed(range(STEPS)):
        _, pullback = jax.vjp(lambda grid: advance(grid, rates, flux_mats), padded_states[section])
        cotangent = pullback(adjoint_now)[0]
        x_ghosts, y_ghosts, z_ghosts = side_pairs(
            [ghost_layer(cotangent, side) for side in range(6)]
        )
        incoming = gather_step(
            (
                lax.all_gather(x_ghosts, "space", axis=0, tiled=True),
                lax.all_gather(y_ghosts, "space", axis=0, tiled=True),
                lax.all_gather(z_ghosts, "space", axis=0, tiled=True),
            )
        )
        adjoint_now = cotangent[:, 1:-1, 1:-1, 1:-1]
        for side in range(6):
            adjoint_now = add_layer(adjoint_now, side, reorient(incoming[side], flips[side]))
    return (adjoint_now[None, None], state[None])


def solution(mesh):
    return jax.shard_map(
        on_device,
        mesh=mesh,
        in_specs=(
            P("space", None, "ckpt", None, None),
            P("ckpt", "space", None, None, None, None),
            P("space", None, None, None),
            P(),
            P(),
            P(),
            P(),
        ),
        out_specs=(P("ckpt", "space", None, None, None, None), P("space", None, None, None, None)),
        check_vma=False,
    )
```

profile of v0, /device:TPU:0, one launch (start us, length us, event | category | flops | bytes accessed | tf_op | source)
XLA Modules:
  0.0 1620.6 jit_solution(11246195897142510362)
XLA Ops:
  8.2 11.1 all_gather.39
  42.4 149.0 %all-gather.2 = f32[64,6,16,16]{3,2,1,0:T(8,128)S(1)} all-gather(f32[2,6,16,16]{3,2,1,0:T(8,128)S(1)} %pad_maximum_fusion.2), channel_id=4, replica_groups=mesh['ckpt'=4,'space'=32] {'space'}, dimensions={0}, use_global_device_ids=true | all-gather | bytes 405504 | tf_op jit(solution)/shard_map/all_gather | solution.py:126
  202.7 139.0 %all-gather.21.cloned.1.call-done = f32[64,6,16,128]{3,2,1,0:T(8,128)} async-done(((f32[2,6,16,128]{3,2,1,0:T(8,128)}), f32[64,6,16,128]{3,2,1,0:T(8,128)}) %all-gather.21.cloned.1.call-update) | async-done | bytes 3145744 | tf_op jit(solution)/shard_map/all_gather | solution.py:124
  351.3 3.2 scatter.41
  354.6 19.7 %scatter.44 = f32[6,18,18,130]{3,2,0,1:T(8,128)S(1)} dynamic-update-slice(f32[6,18,18,130]{3,2,0,1:T(8,128)S(1)} %scatter.41, f32[6,16,1,128]{3,2,0,1:T(1,128)} %copy.1412, s32[]{:T(128)} %constant.830.clone.1, s32[]{:T(128)} %constant.831.clone.1, s32[]{:T(128)} %constant.834.clone.1, s32[]{:T(128)} %constant.831.clone.1) | dynamic-update-slice | bytes 98308 | tf_op jit(solution)/shard_map/scatter | solution.py:30
  374.2 19.7 %scatter.45 = f32[6,18,18,130]{3,2,0,1:T(8,128)S(1)} dynamic-update-slice(f32[6,18,18,130]{3,2,0,1:T(8,128)S(1)} %scatter.44, f32[6,16,1,128]{3,2,0,1:T(1,128)} %copy.1414, s32[]{:T(128)} %constant.830.clone.1, s32[]{:T(128)} %constant.831.clone.1, s32[]{:T(128)} %constant.830.clone.1, s32[]{:T(128)} %constant.831.clone.1) | dynamic-update-slice | bytes 98308 | tf_op jit(solution)/shard_map/scatter | solution.py:30
  393.9 23.4 %scatter.46 = f32[6,18,18,130]{3,2,0,1:T(8,128)S(1)} dynamic-update-slice(f32[6,18,18,130]{3,2,0,1:T(8,128)S(1)} %scatter.45, f32[6,16,16,1]{3,2,0,1:T(8,128)} %copy.1417, s32[]{:T(128)} %constant.830.clone.1, s32[]{:T(128)} %constant.831.clone.1, s32[]{:T(128)} %constant.831.clone.1, s32[]{:T(128)} %constant.835.clone.1) | dynamic-update-slice | bytes 12292 | tf_op jit(solution)/shard_map/scatter | solution.py:32
  417.4 12.1 scatter.49
  444.4 3.4 pad.200
  452.7 151.3 %all-gather.5 = f32[64,6,16,16]{3,2,1,0:T(8,128)S(1)} all-gather(f32[2,6,16,16]{3,2,1,0:T(8,128)S(1)} %pad_maximum_fusion.5), channel_id=7, replica_groups=mesh['ckpt'=4,'space'=32] {'space'}, dimensions={0}, use_global_device_ids=true | all-gather | bytes 405504 | tf_op jit(solution)/shard_map/all_gather | solution.py:126
  621.3 147.7 %all-gather.25.cloned.1.call-done = f32[64,6,16,128]{3,2,1,0:T(8,128)} async-done(((f32[2,6,16,128]{3,2,1,0:T(8,128)}), f32[64,6,16,128]{3,2,1,0:T(8,128)}) %all-gather.25.cloned.1.call-update) | async-done | bytes 3145744 | tf_op jit(solution)/shard_map/all_gather | solution.py:124
  776.7 3.7 scatter.50
  780.4 3.7 scatter.51
  784.1 18.2 %scatter.54 = f32[6,18,18,130]{3,2,0,1:T(8,128)} dynamic-update-slice(f32[6,18,18,130]{3,2,0,1:T(8,128)} %scatter.51, f32[6,16,1,128]{3,2,0,1:T(1,128)} %copy.1436, s32[]{:T(128)} %constant.830.clone.1, s32[]{:T(128)} %constant.831.clone.1, s32[]{:T(128)} %constant.834.clone.1, s32[]{:T(128)} %constant.831.clone.1) | dynamic-update-slice | bytes 98308 | tf_op jit(solution)/shard_map/scatter | solution.py:30
  802.3 18.2 %scatter.55 = f32[6,18,18,130]{3,2,0,1:T(8,128)} dynamic-update-slice(f32[6,18,18,130]{3,2,0,1:T(8,128)} %scatter.54, f32[6,16,1,128]{3,2,0,1:T(1,128)} %copy.1438, s32[]{:T(128)} %constant.830.clone.1, s32[]{:T(128)} %constant.831.clone.1, s32[]{:T(128)} %constant.830.clone.1, s32[]{:T(128)} %constant.831.clone.1) | dynamic-update-slice | bytes 98308 | tf_op jit(solution)/shard_map/scatter | solution.py:30
  820.4 18.2 %scatter.56 = f32[6,18,18,130]{3,2,0,1:T(8,128)} dynamic-update-slice(f32[6,18,18,130]{3,2,0,1:T(8,128)} %scatter.55, f32[6,16,16,1]{3,2,0,1:T(8,128)} %copy.1442, s32[]{:T(128)} %constant.830.clone.1, s32[]{:T(128)} %constant.831.clone.1, s32[]{:T(128)} %constant.831.clone.1, s32[]{:T(128)} %constant.835.clone.1) | dynamic-update-slice | bytes 12292 | tf_op jit(solution)/shard_map/scatter | solution.py:32
  838.6 6.2 scatter.59
  844.8 2.9 add_multiply_fusion
  847.7 2.8 fusion
  856.0 2.8 fusion.4
  879.2 146.6 %all-gather.8 = f32[64,6,16,16]{3,2,1,0:T(8,128)S(1)} all-gather(f32[2,6,16,16]{3,2,1,0:T(8,128)S(1)} %pad_maximum_fusion.8), channel_id=10, replica_groups=mesh['ckpt'=4,'space'=32] {'space'}, dimensions={0}, use_global_device_ids=true | all-gather | bytes 405504 | tf_op jit(solution)/shard_map/all_gather | solution.py:148
  1043.0 4.0 pad_add_fusion.3
  1062.6 132.1 %all-gather.29.cloned.1.call-done = f32[64,6,16,128]{3,2,1,0:T(8,128)} async-done(((f32[2,6,16,128]{3,2,1,0:T(8,128)}), f32[64,6,16,128]{3,2,1,0:T(8,128)}) %all-gather.29.cloned.1.call-update) | async-done | bytes 3145744 | tf_op jit(solution)/shard_map/all_gather | solution.py:146
  1194.7 2.8 fusion.31
  1219.4 9.4 scatter-add.46
  1231.0 3.8 scatter-add.49
  1256.0 142.5 %all-gather.11 = f32[64,6,16,16]{3,2,1,0:T(8,128)S(1)} all-gather(f32[2,6,16,16]{3,2,1,0:T(8,128)S(1)} %pad_maximum_fusion.11), channel_id=13, replica_groups=mesh['ckpt'=4,'space'=32] {'space'}, dimensions={0}, use_global_device_ids=true | all-gather | bytes 405504 | tf_op jit(solution)/shard_map/all_gather | solution.py:148
  1415.7 3.3 pad_add_fusion
  1420.3 2.8 fusion.15
  1434.6 134.8 %all-gather.33.cloned.1.call-done = f32[64,6,16,128]{3,2,1,0:T(8,128)} async-done(((f32[2,6,16,128]{3,2,1,0:T(8,128)}), f32[64,6,16,128]{3,2,1,0:T(8,128)}) %all-gather.33.cloned.1.call-update) | async-done | bytes 3145744 | tf_op jit(solution)/shard_map/all_gather | solution.py:146
  1593.2 12.2 scatter-add.56
  1606.8 5.8 scatter-add.59
  (370 shorter events, 233.1 us)
Async XLA Ops:
  7.2 13.7 copy-start.55
  7.2 15.0 copy-start.54
  7.2 15.0 copy-start.53
  7.2 191.8 %all-gather.23.cloned.1.call-start = ((), (), s32[]{:S(2)}) async-start(), calls=%async_computation.1 | async-start | bytes 3244032 | tf_op jit(solution)/shard_map/all_gather | solution.py:125
  20.1 321.7 %all-gather.21.cloned.1.call-start = ((), (), s32[]{:S(2)}) async-start(), calls=%async_computation | async-start | bytes 3244032 | tf_op jit(solution)/shard_map/all_gather | solution.py:124
  20.8 592.2 %all-gather.27.cloned.1.call-start = ((), (), s32[]{:S(2)}) async-start(), calls=%async_computation.3 | async-start | bytes 3244032 | tf_op jit(solution)/shard_map/all_gather | solution.py:125
  41.7 149.7 %copy-start.41 = (f32[32]{0:T(128)}, f32[32]{0:T(128)S(1)}, u32[]{:S(2)}) copy-start(f32[32]{0:T(128)S(1)} %compare_convert_fusion) | copy-start | bytes 388
  42.4 149.0 %copy-start.45 = (f32[32]{0:T(128)}, f32[32]{0:T(128)S(1)}, u32[]{:S(2)}) copy-start(f32[32]{0:T(128)S(1)} %compare_convert_fusion.1) | copy-start | bytes 388
  195.0 3.3 copy-start.38
  196.4 145.3 %copy-start.49 = (f32[32]{0:T(128)}, f32[32]{0:T(128)S(1)}, u32[]{:S(2)}) copy-start(f32[32]{0:T(128)S(1)} %compare_convert_fusion.4) | copy-start | bytes 388
  197.1 144.6 %copy-start.51 = (f32[32]{0:T(128)}, f32[32]{0:T(128)S(1)}, u32[]{:S(2)}) copy-start(f32[32]{0:T(128)S(1)} %compare_convert_fusion.5) | copy-start | bytes 388
  343.9 73.4 %copy-start.15 = (f32[6,16,16,1]{3,2,0,1:T(8,128)S(1)}, f32[6,16,16,1]{3,2,0,1:T(8,128)}, u32[]{:S(2)}) copy-start(f32[6,16,16,1]{3,2,0,1:T(8,128)} %copy.1418) | copy-start | bytes 18436
  430.9 5.9 copy-start.24
  433.4 3.9 copy-start.22
  442.5 326.5 %all-gather.25.cloned.1.call-start = ((), (), s32[]{:S(2)}) async-start(), calls=%async_computation.2 | async-start | bytes 3244032 | tf_op jit(solution)/shard_map/all_gather | solution.py:124
  444.1 604.2 %all-gather.31.cloned.1.call-start = ((), (), s32[]{:S(2)}) async-start(), calls=%async_computation.5 | async-start | bytes 3244032 | tf_op jit(solution)/shard_map/all_gather | solution.py:147
  444.3 3.4 copy-start.8
  452.7 151.3 %copy-start.42 = (f32[32]{0:T(128)S(1)}, f32[32]{0:T(128)}, u32[]{:S(2)}) copy-start(f32[32]{0:T(128)} %copy-done.41) | copy-start | bytes 388
  452.7 151.3 %copy-start.46 = (f32[32]{0:T(128)S(1)}, f32[32]{0:T(128)}, u32[]{:S(2)}) copy-start(f32[32]{0:T(128)} %copy-done.45) | copy-start | bytes 388
  864.8 3.7 copy-start.1
  870.0 324.6 %all-gather.29.cloned.1.call-start = ((), (), s32[]{:S(2)}) async-start(), calls=%async_computation.4 | async-start | bytes 3244032 | tf_op jit(solution)/shard_map/all_gather | solution.py:146
  870.8 549.5 %all-gather.35.cloned.1.call-start = ((), (), s32[]{:S(2)}) async-start(), calls=%async_computation.7 | async-start | bytes 3244032 | tf_op jit(solution)/shard_map/all_gather | solution.py:147
  879.2 146.6 %copy-start.43 = (f32[32]{0:T(128)S(1)}, f32[32]{0:T(128)}, u32[]{:S(2)}) copy-start(f32[32]{0:T(128)} %copy-done.41) | copy-start | bytes 388
  879.2 146.6 %copy-start.47 = (f32[32]{0:T(128)S(1)}, f32[32]{0:T(128)}, u32[]{:S(2)}) copy-start(f32[32]{0:T(128)} %copy-done.45) | copy-start | bytes 388
  1216.8 12.0 copy-start.17
  1243.3 3.8 copy-start.25
  1251.5 317.9 %all-gather.33.cloned.1.call-start = ((), (), s32[]{:S(2)}) async-start(), calls=%async_computation.6 | async-start | bytes 3244032 | tf_op jit(solution)/shard_map/all_gather | solution.py:146
  1256.0 142.5 %copy-start.44 = (f32[32]{0:T(128)S(1)}, f32[32]{0:T(128)}, u32[]{:S(2)}) copy-start(f32[32]{0:T(128)} %copy-done.41) | copy-start | bytes 388
  1256.0 142.5 %copy-start.48 = (f32[32]{0:T(128)S(1)}, f32[32]{0:T(128)}, u32[]{:S(2)}) copy-start(f32[32]{0:T(128)} %copy-done.45) | copy-start | bytes 388
  1420.3 149.2 %copy-start.50 = (f32[32]{0:T(128)S(1)}, f32[32]{0:T(128)}, u32[]{:S(2)}) copy-start(f32[32]{0:T(128)} %copy-done.49) | copy-start | bytes 388
  1420.3 149.2 %copy-start.52 = (f32[32]{0:T(128)S(1)}, f32[32]{0:T(128)}, u32[]{:S(2)}) copy-start(f32[32]{0:T(128)} %copy-done.51) | copy-start | bytes 388
  1591.4 14.0 copy-start.16
  (32 other events, 50.6 us)
Sparse Core Ops, SparseCore 0:
  20.2 163.9 all-gather.22
  185.8 155.8 all-gather.20
  442.6 169.6 all-gather.26
  613.8 155.1 all-gather.24
  870.1 164.8 all-gather.30
  1036.5 158.0 all-gather.28
  1251.6 165.3 all-gather.34
  1418.7 150.6 all-gather.32
where the time goes:
time: 1630 us; the launch traced here: 1620 us
  blocking collectives  600 us (37%)
  waiting for transfers between devices  554 us (34%)
  local copies, waits for them, and re-layouts  287 us (18%)
  other arithmetic  127 us (8%)
  between operations  31.1 us (2%)
  matrix products  21 us (1%)
    all_gather x2, blocking collectives, fetch(): lax.all_gather(z_faces, 'space', axis=0, tiled=True)  300 us
    all_gather x2, blocking collectives, on_device(): lax.all_gather(z_ghosts, 'space', axis=0, tiled=True)  289 us
    all_gather x2, waiting for transfers between devices, fetch(): lax.all_gather(x_faces, 'space', axis=0, tiled=True)  287 us
    all_gather x2, waiting for transfers between devices, on_device(): lax.all_gather(x_ghosts, 'space', axis=0, tiled=True)  267 us
    scatter x4, local copies, waits for them, and re-layouts, pad_with(): padded = padded.at[:, 1:-1, location, 1:-1].set(ghosts[side])  75.7 us
    scatter x4, local copies, waits for them, and re-layouts, pad_with(): padded = padded.at[:, 1:-1, 1:-1, location].set(ghosts[side])  59.9 us
  transfers between devices with their start and end apart: 8, of which 4 were waited for; matrix products, arithmetic and copies ran while one was open for 8% of the time, Pallas kernels for 0%

commit v1 on v0

--- a/solution.py
+++ b/solution.py
@@ -121,7 +121,10 @@
         x_faces, y_faces, z_faces = side_pairs(layers)
         whole = gather_step(
             (
-                lax.all_gather(x_faces, "space", axis=0, tiled=True),
+                jnp.concatenate(
+                    lax.all_to_all(jnp.stack([x_faces] * lax.axis_size("space")), "space", 0, 0),
+                    axis=0,
+                ),
                 lax.all_gather(y_faces, "space", axis=0, tiled=True),
                 lax.all_gather(z_faces, "space", axis=0, tiled=True),
             )

time: 1630 us -> 1430 us (0.88)
  waiting for transfers between devices: 554 us -> 263 us
  blocking collectives: 600 us -> 670 us
  starting transfers between devices: 0.55 us -> 24.4 us
    all_gather x2 -> x0, waiting for transfers between devices: 287 us -> none  [fetch(): lax.all_gather(x_faces, 'space', axis=0, tiled=True)]
    all_gather x2, blocking collectives: 300 us -> 356 us  [fetch(): lax.all_gather(z_faces, 'space', axis=0, tiled=True)]
    all_to_all x0 -> x2, starting transfers between devices: none -> 24 us  [fetch(): lax.all_to_all(jnp.stack([x_faces] * lax.axis_size('space')), 'space', 0, 0)]
  transfers between devices with their start and end apart: 8 -> 8, of which waited for: 4 -> 2; matrix products, arithmetic and copies ran while one was open for 8% -> 10% of each run, Pallas kernels for 0% -> 0%
where the time goes in v1:
time: 1430 us; the launch traced here: 1420 us
  blocking collectives  670 us (47%)
  local copies, waits for them, and re-layouts  294 us (21%)
  waiting for transfers between devices  263 us (18%)
  other arithmetic  121 us (8%)
  between operations  31.1 us (2%)
  starting transfers between devices  24.4 us (2%)
  matrix products  21 us (1%)
    all_gather x2, blocking collectives, fetch(): lax.all_gather(z_faces, 'space', axis=0, tiled=True)  356 us
    all_gather x2, blocking collectives, on_device(): lax.all_gather(z_ghosts, 'space', axis=0, tiled=True)  303 us
    all_gather x2, waiting for transfers between devices, on_device(): lax.all_gather(x_ghosts, 'space', axis=0, tiled=True)  263 us
    scatter x4, local copies, waits for them, and re-layouts, pad_with(): padded = padded.at[:, 1:-1, location, 1:-1].set(ghosts[side])  76.3 us
    scatter x4, local copies, waits for them, and re-layouts, pad_with(): padded = padded.at[:, 1:-1, 1:-1, location].set(ghosts[side])  59.8 us
    scatter-add x4, local copies, waits for them, and re-layouts, add_layer(): return field.at[:, :, :, location].add(layer)  31.2 us
  transfers between devices with their start and end apart: 8, of which 2 were waited for; matrix products, arithmetic and copies ran while one was open for 10% of the time, Pallas kernels for 0%

profile of v1, /device:TPU:0, one launch (start us, length us, event | category | flops | bytes accessed | tf_op | source)
XLA Modules:
  0.0 1424.3 jit_solution(16430721316513946912)
XLA Ops:
  8.2 11.1 all_gather.33
  22.1 8.0 all-to-all-start
  51.6 175.5 %all-gather.1 = f32[64,6,16,16]{3,2,1,0:T(8,128)S(1)} all-gather(f32[2,6,16,16]{3,2,1,0:T(8,128)S(1)} %pad_maximum_fusion.2), channel_id=3, replica_groups=mesh['ckpt'=4,'space'=32] {'space'}, dimensions={0}, use_global_device_ids=true | all-gather | bytes 405504 | tf_op jit(solution)/shard_map/all_gather | solution.py:129
  248.7 19.9 %scatter.44 = f32[6,18,18,130]{3,2,0,1:T(8,128)S(1)} dynamic-update-slice(f32[6,18,18,130]{3,2,0,1:T(8,128)S(1)} %scatter.41, f32[6,16,1,128]{3,2,0,1:T(1,128)S(1)} %copy.1445, s32[]{:T(128)} %constant.830.clone.1, s32[]{:T(128)} %constant.831.clone.1, s32[]{:T(128)} %constant.834.clone.1, s32[]{:T(128)} %constant.831.clone.1) | dynamic-update-slice | bytes 98308 | tf_op jit(solution)/shard_map/scatter | solution.py:30
  268.6 19.7 %scatter.45 = f32[6,18,18,130]{3,2,0,1:T(8,128)S(1)} dynamic-update-slice(f32[6,18,18,130]{3,2,0,1:T(8,128)S(1)} %scatter.44, f32[6,16,1,128]{3,2,0,1:T(1,128)} %copy.1447, s32[]{:T(128)} %constant.830.clone.1, s32[]{:T(128)} %constant.831.clone.1, s32[]{:T(128)} %constant.830.clone.1, s32[]{:T(128)} %constant.831.clone.1) | dynamic-update-slice | bytes 98308 | tf_op jit(solution)/shard_map/scatter | solution.py:30
  288.3 23.4 %scatter.46 = f32[6,18,18,130]{3,2,0,1:T(8,128)S(1)} dynamic-update-slice(f32[6,18,18,130]{3,2,0,1:T(8,128)S(1)} %scatter.45, f32[6,16,16,1]{3,2,0,1:T(8,128)} %copy.1450, s32[]{:T(128)} %constant.830.clone.1, s32[]{:T(128)} %constant.831.clone.1, s32[]{:T(128)} %constant.831.clone.1, s32[]{:T(128)} %constant.835.clone.1) | dynamic-update-slice | bytes 12292 | tf_op jit(solution)/shard_map/scatter | solution.py:32
  311.7 12.1 scatter.49
  339.8 16.0 %all-to-all-start.1 = ((f32[32,1,2,6,16,128]{5,4,3,2,1,0:T(8,128)}), f32[32,1,2,6,16,128]{5,4,3,2,1,0:T(8,128)}, u32[]{:S(2)}, u32[]{:S(2)}) async-start(f32[32,1,2,6,16,128]{5,4,3,2,1,0:T(8,128)} %stack.47), calls=%async_computation.1 | async-start | bytes 6291456 | tf_op jit(solution)/shard_map/all_to_all | solution.py:125
  356.0 3.4 pad.200
  364.3 180.4 %all-gather.3 = f32[64,6,16,16]{3,2,1,0:T(8,128)S(1)} all-gather(f32[2,6,16,16]{3,2,1,0:T(8,128)S(1)} %pad_maximum_fusion.5), channel_id=5, replica_groups=mesh['ckpt'=4,'space'=32] {'space'}, dimensions={0}, use_global_device_ids=true | all-gather | bytes 405504 | tf_op jit(solution)/shard_map/all_gather | solution.py:129
  561.7 3.7 scatter.50
  566.2 3.7 scatter.51
  577.7 18.6 %scatter.54 = f32[6,18,18,130]{3,2,0,1:T(8,128)} dynamic-update-slice(f32[6,18,18,130]{3,2,0,1:T(8,128)} %scatter.51, f32[6,16,1,128]{3,2,0,1:T(1,128)S(1)} %copy.1468, s32[]{:T(128)} %constant.830.clone.1, s32[]{:T(128)} %constant.831.clone.1, s32[]{:T(128)} %constant.834.clone.1, s32[]{:T(128)} %constant.831.clone.1) | dynamic-update-slice | bytes 98308 | tf_op jit(solution)/shard_map/scatter | solution.py:30
  596.3 18.1 %scatter.55 = f32[6,18,18,130]{3,2,0,1:T(8,128)} dynamic-update-slice(f32[6,18,18,130]{3,2,0,1:T(8,128)} %scatter.54, f32[6,16,1,128]{3,2,0,1:T(1,128)} %copy.1470, s32[]{:T(128)} %constant.830.clone.1, s32[]{:T(128)} %constant.831.clone.1, s32[]{:T(128)} %constant.830.clone.1, s32[]{:T(128)} %constant.831.clone.1) | dynamic-update-slice | bytes 98308 | tf_op jit(solution)/shard_map/scatter | solution.py:30
  614.5 18.2 %scatter.56 = f32[6,18,18,130]{3,2,0,1:T(8,128)} dynamic-update-slice(f32[6,18,18,130]{3,2,0,1:T(8,128)} %scatter.55, f32[6,16,16,1]{3,2,0,1:T(8,128)} %copy.1474, s32[]{:T(128)} %constant.830.clone.1, s32[]{:T(128)} %constant.831.clone.1, s32[]{:T(128)} %constant.831.clone.1, s32[]{:T(128)} %constant.835.clone.1) | dynamic-update-slice | bytes 12292 | tf_op jit(solution)/shard_map/scatter | solution.py:32
  632.7 6.1 scatter.59
  638.8 2.9 add_multiply_fusion
  641.7 2.8 fusion
  650.0 2.8 fusion.4
  673.2 154.9 %all-gather.6 = f32[64,6,16,16]{3,2,1,0:T(8,128)S(1)} all-gather(f32[2,6,16,16]{3,2,1,0:T(8,128)S(1)} %pad_maximum_fusion.8), channel_id=8, replica_groups=mesh['ckpt'=4,'space'=32] {'space'}, dimensions={0}, use_global_device_ids=true | all-gather | bytes 405504 | tf_op jit(solution)/shard_map/all_gather | solution.py:151
  845.2 4.0 pad_add_fusion.3
  864.7 129.9 %all-gather.21.cloned.1.call-done = f32[64,6,16,128]{3,2,1,0:T(8,128)} async-done(((f32[2,6,16,128]{3,2,1,0:T(8,128)}), f32[64,6,16,128]{3,2,1,0:T(8,128)}) %all-gather.21.cloned.1.call-update) | async-done | bytes 3145744 | tf_op jit(solution)/shard_map/all_gather | solution.py:149
  994.7 2.8 fusion.31
  1019.4 9.4 scatter-add.46
  1031.0 3.8 scatter-add.49
  1056.0 148.1 %all-gather.9 = f32[64,6,16,16]{3,2,1,0:T(8,128)S(1)} all-gather(f32[2,6,16,16]{3,2,1,0:T(8,128)S(1)} %pad_maximum_fusion.11), channel_id=11, replica_groups=mesh['ckpt'=4,'space'=32] {'space'}, dimensions={0}, use_global_device_ids=true | all-gather | bytes 405504 | tf_op jit(solution)/shard_map/all_gather | solution.py:151
  1221.3 3.3 pad_add_fusion
  1225.9 2.8 fusion.15
  1240.3 132.8 %all-gather.25.cloned.1.call-done = f32[64,6,16,128]{3,2,1,0:T(8,128)} async-done(((f32[2,6,16,128]{3,2,1,0:T(8,128)}), f32[64,6,16,128]{3,2,1,0:T(8,128)}) %all-gather.25.cloned.1.call-update) | async-done | bytes 3145744 | tf_op jit(solution)/shard_map/all_gather | solution.py:149
  1373.1 2.8 fusion.19
  1396.9 12.2 scatter-add.56
  1410.5 5.8 scatter-add.59
  (376 shorter events, 234.2 us)
Async XLA Ops:
  7.2 235.1 %all-gather.17.cloned.1.call-start = ((), (), s32[]{:S(2)}) async-start(), calls=%async_computation.2 | async-start | bytes 3244032 | tf_op jit(solution)/shard_map/all_gather | solution.py:128
  22.1 8.1 copy-start.57
  22.1 9.4 copy-start.55
  22.1 9.4 copy-start.56
  22.1 212.5 %all-to-all-start = ((f32[32,1,2,6,16,128]{5,4,3,2,1,0:T(8,128)}), f32[32,1,2,6,16,128]{5,4,3,2,1,0:T(8,128)}, u32[]{:S(2)}, u32[]{:S(2)}) async-start(f32[32,1,2,6,16,128]{5,4,3,2,1,0:T(8,128)} %stack.43), calls=%async_computation | async-start | bytes 6291456 | tf_op jit(solution)/shard_map/all_to_all | solution.py:125
  30.1 539.8 %all-gather.19.cloned.1.call-start = ((), (), s32[]{:S(2)}) async-start(), calls=%async_computation.3 | async-start | bytes 3244032 | tf_op jit(solution)/shard_map/all_gather | solution.py:128
  50.9 176.2 %copy-start.41 = (f32[32]{0:T(128)}, f32[32]{0:T(128)S(1)}, u32[]{:S(2)}) copy-start(f32[32]{0:T(128)S(1)} %compare_convert_fusion) | copy-start | bytes 388
  51.5 175.5 %copy-start.45 = (f32[32]{0:T(128)}, f32[32]{0:T(128)S(1)}, u32[]{:S(2)}) copy-start(f32[32]{0:T(128)S(1)} %compare_convert_fusion.1) | copy-start | bytes 388
  232.0 4.8 copy-start.49
  232.7 4.1 copy-start.52
  233.9 8.3 copy-start.39
  244.4 67.2 %copy-start.15 = (f32[6,16,16,1]{3,2,0,1:T(8,128)S(1)}, f32[6,16,16,1]{3,2,0,1:T(8,128)}, u32[]{:S(2)}) copy-start(f32[6,16,16,1]{3,2,0,1:T(8,128)} %copy.1451) | copy-start | bytes 18436
  325.2 5.9 copy-start.24
  327.8 3.9 copy-start.22
  339.8 214.0 %all-to-all-start.1 = ((f32[32,1,2,6,16,128]{5,4,3,2,1,0:T(8,128)}), f32[32,1,2,6,16,128]{5,4,3,2,1,0:T(8,128)}, u32[]{:S(2)}, u32[]{:S(2)}) async-start(f32[32,1,2,6,16,128]{5,4,3,2,1,0:T(8,128)} %stack.47), calls=%async_computation.1 | async-start | bytes 6291456 | tf_op jit(solution)/shard_map/all_to_all | solution.py:125
  355.7 494.7 %all-gather.23.cloned.1.call-start = ((), (), s32[]{:S(2)}) async-start(), calls=%async_computation.5 | async-start | bytes 3244032 | tf_op jit(solution)/shard_map/all_gather | solution.py:150
  356.0 3.4 copy-start.8
  364.3 180.4 %copy-start.42 = (f32[32]{0:T(128)S(1)}, f32[32]{0:T(128)}, u32[]{:S(2)}) copy-start(f32[32]{0:T(128)} %copy-done.41) | copy-start | bytes 388
  364.3 180.4 %copy-start.46 = (f32[32]{0:T(128)S(1)}, f32[32]{0:T(128)}, u32[]{:S(2)}) copy-start(f32[32]{0:T(128)} %copy-done.45) | copy-start | bytes 388
  658.8 3.7 copy-start.1
  664.0 330.7 %all-gather.21.cloned.1.call-start = ((), (), s32[]{:S(2)}) async-start(), calls=%async_computation.4 | async-start | bytes 3244032 | tf_op jit(solution)/shard_map/all_gather | solution.py:149
  664.8 561.1 %all-gather.27.cloned.1.call-start = ((), (), s32[]{:S(2)}) async-start(), calls=%async_computation.7 | async-start | bytes 3244032 | tf_op jit(solution)/shard_map/all_gather | solution.py:150
  673.2 154.9 %copy-start.43 = (f32[32]{0:T(128)S(1)}, f32[32]{0:T(128)}, u32[]{:S(2)}) copy-start(f32[32]{0:T(128)} %copy-done.41) | copy-start | bytes 388
  673.2 154.9 %copy-start.47 = (f32[32]{0:T(128)S(1)}, f32[32]{0:T(128)}, u32[]{:S(2)}) copy-start(f32[32]{0:T(128)} %copy-done.45) | copy-start | bytes 388
  1016.8 12.0 copy-start.17
  1043.3 3.8 copy-start.25
  1051.5 321.5 %all-gather.25.cloned.1.call-start = ((), (), s32[]{:S(2)}) async-start(), calls=%async_computation.6 | async-start | bytes 3244032 | tf_op jit(solution)/shard_map/all_gather | solution.py:149
  1056.0 148.1 %copy-start.44 = (f32[32]{0:T(128)S(1)}, f32[32]{0:T(128)}, u32[]{:S(2)}) copy-start(f32[32]{0:T(128)} %copy-done.41) | copy-start | bytes 388
  1056.0 148.1 %copy-start.48 = (f32[32]{0:T(128)S(1)}, f32[32]{0:T(128)}, u32[]{:S(2)}) copy-start(f32[32]{0:T(128)} %copy-done.45) | copy-start | bytes 388
  1225.9 147.2 %copy-start.51 = (f32[32]{0:T(128)S(1)}, f32[32]{0:T(128)}, u32[]{:S(2)}) copy-start(f32[32]{0:T(128)} %copy-done.49) | copy-start | bytes 388
  1225.9 147.2 %copy-start.54 = (f32[32]{0:T(128)S(1)}, f32[32]{0:T(128)}, u32[]{:S(2)}) copy-start(f32[32]{0:T(128)} %copy-done.52) | copy-start | bytes 388
  1395.1 14.0 copy-start.16
  (34 other events, 57.4 us)
Sparse Core Ops, SparseCore 0:
  20.1 209.1 all-gather.16
  337.0 204.4 all-gather.18
  664.1 169.3 all-gather.22
  835.0 159.6 all-gather.20
  1051.6 165.5 all-gather.26
  1218.7 154.3 all-gather.24
